TPU v7x, 512 devices: a whole 4x8x8 slice. The times are simulated.
512 devices in a mesh: expert: 16 (over z, core), tensor: 32 (over x, y).
Axes of the slice: x: 4, y: 8, z: 8, core: 2. Of those that a mesh axis runs over, the one named last changes fastest.
Arguments:
- tokens: bfloat16 [2048, 5120], P('expert', 'tensor'), may hold values from -6 to 6
- routes: int32 [2048, 6], P('expert'), may hold values from 0 to 15, all different within a row; in each aligned block of 128 rows (0 to 127, 128 to 255, ...) at most 64 rows name the same one
- gates: float32 [2048, 6], P('expert'), may hold values from 0.05 to 0.35
- w_gate: bfloat16 [16, 1536, 5120], P('expert', 'tensor'), may hold values from -0.078125 to 0.078125
- w_up: bfloat16 [16, 1536, 5120], P('expert', 'tensor'), may hold values from -0.078125 to 0.078125
- w_down: bfloat16 [16, 1536, 5120], P('expert', None, 'tensor'), may hold values from -0.15625 to 0.15625
- shared_gate: bfloat16 [1536, 5120], P('tensor'), may hold values from -0.078125 to 0.078125
- shared_up: bfloat16 [1536, 5120], P('tensor'), may hold values from -0.078125 to 0.078125
- shared_down: bfloat16 [1536, 5120], P(None, 'tensor'), may hold values from -0.15625 to 0.15625
- vocab: bfloat16 [65536, 5120], P(('expert', 'tensor'))
- targets: int32 [64], replicated, may hold values from 0 to 65535
Outputs:
- layer_out: bfloat16 [2048, 5120], P('expert', 'tensor')
- loglik: float32 [64], replicated
Inputs may be any that keep to these rules, and one draw needn't show every extreme that they name: `routes`: the tokens of one group name one expert at most 64 times; in every draw some group names some expert exactly 64 times.
All inputs are finite; a program needn't handle non-finite values.
Results may differ from a plain program's by a relative error of at most 0.0041.
Values may be sent and summed in bfloat16 or wider, within the bound.
No kernel may reach another device: no remote copies, remote signals or barrier semaphores. Data moves between devices by JAX's collectives and lax.ppermute only.
A program may use at most 64 MiB of HBM per device.

v0:
```python
import jax
import jax.numpy as jnp
from jax import lax
from jax.sharding import PartitionSpec as P

EXPERTS = 16
SCORE_E = 4


def slot_tables(routes, gates, capacity):
    picks = (routes[:, :, None] == jnp.arange(EXPERTS, dtype=jnp.int32)[None, None, :]).astype(
        jnp.int32
    )
    per_token = jnp.sum(picks, axis=1)
    earlier = jnp.cumsum(per_token, axis=0) - per_token
    slots = jnp.sum(picks * earlier[:, None, :], axis=2)
    places = (slots[:, :, None] == jnp.arange(capacity, dtype=jnp.int32)[None, None, :]).astype(
        jnp.float32
    )
    picked = picks.astype(jnp.float32)
    select = jnp.einsum("ikr,iks->rsi", picked, places, precision=lax.Precision.HIGHEST)
    weigh = jnp.einsum("ikr,iks,ik->rsi", picked, places, gates, precision=lax.Precision.HIGHEST)
    return (select.astype(jnp.bfloat16), weigh)


def contract_last(left, right):
    return lax.dot_general(
        left, right, (((1,), (1,)), ((), ())), preferred_element_type=jnp.float32
    )


def shards(
    tokens, routes, gates, w_gate, w_up, w_down, shared_gate, shared_up, shared_down, vocab, targets
):
    tok_rows = tokens.shape[0]
    capacity = tok_rows // 2
    groups = lax.axis_size("expert")
    lanes = lax.axis_size("tensor")
    exp_dev = w_gate.shape[0]
    width = w_gate.shape[1]
    out_width = w_down.shape[2]
    select, weigh = slot_tables(routes, gates, capacity)
    outgoing = jnp.einsum("rsi,id->rsd", select, tokens, preferred_element_type=jnp.float32).astype(
        jnp.bfloat16
    )
    arrived = lax.all_to_all(outgoing, "expert", split_axis=0, concat_axis=1, tiled=True)
    slot_count = arrived.shape[1]
    flat_rows = arrived.reshape(exp_dev * slot_count, arrived.shape[2])
    pieces = (
        lax.all_gather(flat_rows, "tensor", axis=1, tiled=True),
        lax.all_gather(tokens, "tensor", axis=1, tiled=True),
    )
    span = pieces[0].shape[1]
    rows = pieces[0].reshape(exp_dev, slot_count, span)
    gate_acc = jnp.einsum("erw,efw->erf", rows, w_gate, preferred_element_type=jnp.float32)
    up_acc = jnp.einsum("erw,efw->erf", rows, w_up, preferred_element_type=jnp.float32)
    shared_gate_acc = contract_last(pieces[1], shared_gate)
    shared_up_acc = contract_last(pieces[1], shared_up)
    hidden_routed = (jax.nn.silu(gate_acc) * up_acc).astype(jnp.bfloat16)
    hidden_shared = (jax.nn.silu(shared_gate_acc) * shared_up_acc).astype(jnp.bfloat16)
    flat_hidden = hidden_routed.reshape(exp_dev * slot_count, width)
    pieces = (
        lax.all_gather(flat_hidden, "tensor", axis=1, tiled=True),
        lax.all_gather(hidden_shared, "tensor", axis=1, tiled=True),
    )
    span = pieces[0].shape[1]
    rows = pieces[0].reshape(exp_dev, slot_count, span)
    routed_out = jnp.einsum("erw,ewd->erd", rows, w_down, preferred_element_type=jnp.float32)
    shared_out = jnp.dot(pieces[1], shared_down, preferred_element_type=jnp.float32)
    returned = lax.all_to_all(
        routed_out.astype(jnp.bfloat16), "expert", split_axis=1, concat_axis=0, tiled=True
    )
    routed = jnp.einsum(
        "rsi,rsd->id", weigh, returned.astype(jnp.float32), precision=lax.Precision.HIGHEST
    )
    layer_out = (tokens.astype(jnp.float32) + shared_out + routed).astype(jnp.bfloat16)
    scored = layer_out[tok_rows - SCORE_E :].reshape(1, SCORE_E * out_width)
    collected = lax.all_gather(scored, ("expert", "tensor"), axis=0, tiled=True)
    full_rows = (
        collected.reshape(groups, lanes, SCORE_E, out_width)
        .transpose(0, 2, 1, 3)
        .reshape(groups * SCORE_E, lanes * out_width)
    )
    logits = contract_last(full_rows, vocab)
    exp_sums = jnp.sum(jnp.exp(logits), axis=1)
    offset = (lax.axis_index("expert") * lanes + lax.axis_index("tensor")) * vocab.shape[0]
    columns = offset + jnp.arange(vocab.shape[0], dtype=jnp.int32)
    target_part = jnp.sum(jnp.where(targets[:, None] == columns[None, :], logits, 0.0), axis=1)
    totals, target_logit = lax.psum((exp_sums, target_part), ("expert", "tensor"))
    loglik = target_logit - jnp.log(totals)
    return (layer_out, loglik)


def solution(mesh):
    placed = (
        P("expert", "tensor"),
        P("expert", None),
        P("expert", None),
        P("expert", "tensor", None),
        P("expert", "tensor", None),
        P("expert", None, "tensor"),
        P("tensor", None),
        P("tensor", None),
        P(None, "tensor"),
        P(("expert", "tensor"), None),
        P(),
    )
    return jax.shard_map(
        shards, mesh=mesh, in_specs=placed, out_specs=(P("expert", "tensor"), P()), check_vma=False
    )
```

profile of v0, /device:TPU:1, one launch (start us, length us, event | category | flops | bytes accessed | tf_op | source)
XLA Modules:
  0.0 622.9 jit_solution(7036797286087049021)
XLA Ops:
  7.2 0.0 copy-start
  7.2 0.0 all-gather.7.cloned.1.call-start
  7.2 0.9 copy.21
  8.1 0.3 convert_reduce_fusion
  8.4 0.2 reduce_window_sum.11
  8.6 2.4 select_reduce_fusion
  11.0 1.2 fusion
  12.2 0.3 convolution_convert_fusion.1
  12.6 29.1 %all_to_all.21 = bf16[16,64,160]{2,1,0:T(8,128)(2,1)S(1)} all-to-all(bf16[16,64,160]{2,1,0:T(8,128)(2,1)S(1)} %convolution_convert_fusion.1), channel_id=1, replica_groups=mesh['expert'=16,'tensor'=32] {'expert'}, dimensions={0} | all-to-all | bytes 655360 | tf_op jit(solution)/shard_map/all_to_all | solution.py:46
  41.7 0.9 copy.24
  42.6 0.0 all-gather.7.cloned.1.call-update
  42.6 0.0 all-gather.9.cloned.1.call-start
  42.7 110.4 %all-gather.7.cloned.1.call-done = bf16[1024,5120]{0,1:T(8,128)(2,1)} async-done(((bf16[1024,160]{0,1:T(8,128)(2,1)}), bf16[1024,5120]{0,1:T(8,128)(2,1)}) %all-gather.7.cloned.1.call-update) | async-done | bytes 10485776 | tf_op jit(solution)/shard_map/all_gather | solution.py:50
  153.1 6.1 fusion.11
  159.2 0.9 copy-done.1
  160.0 2.6 fusion.2
  162.7 0.0 all-gather.9.cloned.1.call-update
  162.7 0.2 all-gather.5.cloned.1.call-start
  162.9 0.5 all-gather.5.cloned.1.call-update
  163.5 0.1 copy.22
  163.6 2.7 convolution_bitcast_fusion
  166.3 76.0 %all-gather.9.cloned.1.call-done = bf16[1024,1536]{0,1:T(8,128)(2,1)} async-done(((bf16[1024,48]{0,1:T(8,128)(2,1)}), bf16[1024,1536]{0,1:T(8,128)(2,1)}) %all-gather.9.cloned.1.call-update) | async-done | bytes 3145744 | tf_op jit(solution)/shard_map/all_gather | solution.py:63
  242.3 2.6 fusion.1
  244.9 0.8 copy.25
  245.8 0.5 broadcast.28
  246.3 4.0 reduce.1
  250.3 1.5 reshape.84
  251.8 11.8 %all-to-all-start.1 = ((bf16[16,2,5120]{2,1,0:T(2,128)(2,1)}), bf16[16,2,5120]{2,1,0:T(2,128)(2,1)S(1)}, u32[]{:S(2)}, u32[]{:S(2)}) async-start(bf16[16,2,5120]{2,1,0:T(2,128)(2,1)} %reshape.84), calls=%async_computation.1 | async-start | bytes 655360 | tf_op jit(solution)/shard_map/all_to_all | solution.py:70
  263.6 60.0 %all-gather.5.cloned.1.call-done = bf16[128,5120]{0,1:T(8,128)(2,1)} async-done(((bf16[128,160]{0,1:T(8,128)(2,1)}), bf16[128,5120]{0,1:T(8,128)(2,1)}) %all-gather.5.cloned.1.call-update) | async-done | bytes 1310736 | tf_op jit(solution)/shard_map/all_gather | solution.py:51
  323.6 1.8 fusion.21
  325.3 0.4 fusion.5
  325.7 36.5 %all_gather.16 = bf16[128,1536]{0,1:T(8,128)(2,1)S(1)} all-gather(bf16[128,48]{0,1:T(8,128)(2,1)S(1)} %fusion.5), channel_id=1, replica_groups=mesh['expert'=16,'tensor'=32] {'tensor'}, dimensions={1}, use_global_device_ids=true | all-gather | bytes 405504 | tf_op jit(solution)/shard_map/all_gather | solution.py:64
  362.2 0.9 reshape.85
  363.2 0.1 copy.32
  363.2 1.1 copy-done.5
  364.3 1.1 convolution_bitcast_fusion.1
  365.5 0.3 fusion.4
  365.8 0.1 slice.4
  365.9 0.1 copy.29
  366.0 0.1 reshape.76
  366.1 145.7 %all-gather = bf16[512,1,640]{2,1,0:T(2,128)(2,1)S(1)} all-gather(bf16[1,1,640]{2,1,0:T(2,128)(2,1)S(1)} %reshape.76), channel_id=1, replica_groups=mesh['expert'=16,'tensor'=32] {'expert','tensor'}, dimensions={0}, use_global_device_ids=true | all-gather | bytes 656640 | tf_op jit(solution)/shard_map/all_gather | solution.py:78
  511.8 4.0 reduce
  515.8 0.7 reshape.74
  516.5 0.2 copy.30
  516.7 1.7 reshape.75
  518.4 0.7 exponential_reduce_fusion
  519.1 96.8 %all-reduce = (f32[64]{0:T(128)S(1)}, f32[64]{0:T(128)S(1)}) all-reduce(f32[64]{0:T(128)S(1)} %get-tuple-element.3, f32[64]{0:T(128)S(1)} %get-tuple-element.2), channel_id=1, replica_groups=mesh['expert'=16,'tensor'=32] {'expert','tensor'}, use_global_device_ids=true, to_apply=%region_4.5 | all-reduce | flops 128 | bytes 1024 | tf_op jit(solution)/shard_map/psum | solution.py:89
  615.9 0.5 log_subtract_fusion
  (30 shorter events, 0.1 us)
Async XLA Ops:
  7.2 511.2 %copy-start = (bf16[128,5120]{1,0:T(8,128)(2,1)S(1)}, bf16[128,5120]{1,0:T(8,128)(2,1)}, u32[]{:S(2)}) copy-start(bf16[128,5120]{1,0:T(8,128)(2,1)} %param.20) | copy-start | bytes 3932164
  7.2 145.9 %all-gather.7.cloned.1.call-start = ((), (), s32[]{:S(2)}) async-start(), calls=%async_computation.3 | async-start | bytes 10813440 | tf_op jit(solution)/shard_map/all_gather | solution.py:50
  8.4 3.8 copy-start.10
  12.6 140.5 %copy-start.3 = (bf16[1,48,5120]{2,1,0:T(8,128)(2,1)S(1)}, bf16[1,48,5120]{2,1,0:T(8,128)(2,1)}, u32[]{:S(2)}) copy-start(bf16[1,48,5120]{2,1,0:T(8,128)(2,1)} %param.14) | copy-start | bytes 1474564
  42.6 116.5 %copy-start.4 = (bf16[1,48,5120]{2,1,0:T(8,128)(2,1)S(1)}, bf16[1,48,5120]{2,1,0:T(8,128)(2,1)}, u32[]{:S(2)}) copy-start(bf16[1,48,5120]{2,1,0:T(8,128)(2,1)} %param.15) | copy-start | bytes 1474564
  42.6 199.7 %all-gather.9.cloned.1.call-start = ((), (), s32[]{:S(2)}) async-start(), calls=%async_computation.4 | async-start | bytes 3244032 | tf_op jit(solution)/shard_map/all_gather | solution.py:63
  153.1 7.0 %copy-start.1 = (bf16[1024,5120]{0,1:T(8,128)(2,1)S(1)}, bf16[1024,5120]{0,1:T(8,128)(2,1)}, u32[]{:S(2)}) copy-start(bf16[1024,5120]{0,1:T(8,128)(2,1)} %all-gather.7.cloned.1.call-done) | copy-start | bytes 31457284
  160.0 3.4 copy-start.13
  162.7 160.8 %all-gather.5.cloned.1.call-start = ((), (), s32[]{:S(2)}) async-start(), calls=%async_computation.2 | async-start | bytes 1351680 | tf_op jit(solution)/shard_map/all_gather | solution.py:51
  163.6 78.8 %copy-start.8 = (bf16[1,1536,160]{1,2,0:T(8,128)(2,1)S(1)}, bf16[1,1536,160]{1,2,0:T(8,128)(2,1)}, u32[]{:S(2)}) copy-start(bf16[1,1536,160]{1,2,0:T(8,128)(2,1)} %param.16) | copy-start | bytes 1474564
  250.3 73.2 %copy-start.6 = (bf16[48,5120]{1,0:T(8,128)(2,1)S(1)}, bf16[48,5120]{1,0:T(8,128)(2,1)}, u32[]{:S(2)}) copy-start(bf16[48,5120]{1,0:T(8,128)(2,1)} %param.17) | copy-start | bytes 1474564
  251.8 73.5 %copy-start.7 = (bf16[48,5120]{1,0:T(8,128)(2,1)S(1)}, bf16[48,5120]{1,0:T(8,128)(2,1)}, u32[]{:S(2)}) copy-start(bf16[48,5120]{1,0:T(8,128)(2,1)} %param.18) | copy-start | bytes 1474564
  251.8 110.4 %all-to-all-start.1 = ((bf16[16,2,5120]{2,1,0:T(2,128)(2,1)}), bf16[16,2,5120]{2,1,0:T(2,128)(2,1)S(1)}, u32[]{:S(2)}, u32[]{:S(2)}) async-start(bf16[16,2,5120]{2,1,0:T(2,128)(2,1)} %reshape.84), calls=%async_computation.1 | async-start | bytes 655360 | tf_op jit(solution)/shard_map/all_to_all | solution.py:70
  323.6 1.8 copy-start.2
  363.1 1.2 copy-start.5
  363.1 2.4 copy-start.9
  363.1 2.4 copy-start.11
  365.8 150.0 %copy-start.12 = (bf16[128,160]{0,1:T(8,128)(2,1)}, bf16[128,160]{0,1:T(8,128)(2,1)S(1)}, u32[]{:S(2)}) copy-start(bf16[128,160]{0,1:T(8,128)(2,1)S(1)} %fusion.4) | copy-start | bytes 122884
  516.7 1.7 copy-start.14
Sparse Core Ops, SparseCore 0:
  42.7 110.3 all-gather.6
  162.8 79.4 all-gather.8
  245.5 78.0 all-gather.4
where the time goes:
time: 623 us
  blocking collectives  308 us (49%)
  waiting for transfers between devices  247 us (40%)
  matrix products  19.8 us (3%)
  between operations  14.1 us (2%)
  starting transfers between devices  12.1 us (2%)
  other arithmetic  11.4 us (2%)
  local copies, waits for them, and re-layouts  10.7 us (2%)
    all_gather x1, blocking collectives, shards(): collected = lax.all_gather(scored, ('expert', 'tensor'), axis=0, tiled=True)  146 us
    all_gather x1, waiting for transfers between devices, shards(): lax.all_gather(flat_rows, 'tensor', axis=1, tiled=True)  110 us
    psum x1, blocking collectives, shards(): lax.psum((exp_sums, target_part), ('expert', 'tensor'))  96.8 us
    all_gather x1, waiting for transfers between devices, shards(): lax.all_gather(flat_hidden, 'tensor', axis=1, tiled=True)  76 us
    all_gather x1, waiting for transfers between devices, shards(): lax.all_gather(tokens, 'tensor', axis=1, tiled=True)  60 us
    all_gather x1, blocking collectives, shards(): lax.all_gather(hidden_shared, 'tensor', axis=1, tiled=True)  36.5 us
    all_to_all x1, blocking collectives, shards(): lax.all_to_all(outgoing, 'expert', split_axis=0, concat_axis=1, tiled=True)  29.1 us
  transfers between devices with their start and end apart: 4, of which 3 were waited for; matrix products, arithmetic and copies ran while one was open for 2% of the time, Pallas kernels for 0%

commit v1 on v0

--- a/solution.py
+++ b/solution.py
@@ -75,7 +75,12 @@
     )
     layer_out = (tokens.astype(jnp.float32) + shared_out + routed).astype(jnp.bfloat16)
     scored = layer_out[tok_rows - SCORE_E :].reshape(1, SCORE_E * out_width)
-    collected = lax.all_gather(scored, ("expert", "tensor"), axis=0, tiled=True)
+    collected = jnp.concatenate(
+        lax.all_to_all(
+            jnp.stack([scored] * lax.axis_size(("expert", "tensor"))), ("expert", "tensor"), 0, 0
+        ),
+        axis=0,
+    )
     full_rows = (
         collected.reshape(groups, lanes, SCORE_E, out_width)
         .transpose(0, 2, 1, 3)

time: 623 us -> 544 us (0.87)
  blocking collectives: 308 us -> 160 us
  starting transfers between devices: 12.1 us -> 43.2 us
  waiting for transfers between devices: 247 us -> 274 us
    all_gather x1 -> x0, blocking collectives: 146 us -> none  [shards(): collected = lax.all_gather(scored, ('expert', 'tensor'), axis=0, tiled=True)]
    all_to_all x0 -> x1, starting transfers between devices: none -> 31.1 us  [shards(): lax.all_to_all(jnp.stack([scored] * lax.axis_size(('expert', 'tensor'))),...]
    all_to_all x0 -> x1, waiting for transfers between devices: none -> 27.4 us  [shards(): lax.all_to_all(jnp.stack([scored] * lax.axis_size(('expert', 'tensor'))),...]
  transfers between devices with their start and end apart: 4 -> 5, of which waited for: 3 -> 4; matrix products, arithmetic and copies ran while one was open for 2% -> 3% of each run, Pallas kernels for 0% -> 0%
where the time goes in v1:
time: 544 us
  waiting for transfers between devices  274 us (50%)
  blocking collectives  160 us (29%)
  starting transfers between devices  43.2 us (8%)
  matrix products  19.8 us (4%)
  other arithmetic  16.8 us (3%)
  local copies, waits for them, and re-layouts  16.2 us (3%)
  between operations  14.1 us (3%)
    all_gather x1, waiting for transfers between devices, shards(): lax.all_gather(flat_rows, 'tensor', axis=1, tiled=True)  110 us
    psum x1, blocking collectives, shards(): lax.psum((exp_sums, target_part), ('expert', 'tensor'))  93.7 us
    all_gather x1, waiting for transfers between devices, shards(): lax.all_gather(flat_hidden, 'tensor', axis=1, tiled=True)  76 us
    all_gather x1, waiting for transfers between devices, shards(): lax.all_gather(tokens, 'tensor', axis=1, tiled=True)  59.9 us
    all_gather x1, blocking collectives, shards(): lax.all_gather(hidden_shared, 'tensor', axis=1, tiled=True)  36.7 us
    all_to_all x1, starting transfers between devices, shards(): lax.all_to_all(jnp.stack([scored] * lax.axis_size(('expert', 'tensor'))),...  31.1 us
    all_to_all x1, blocking collectives, shards(): lax.all_to_all(outgoing, 'expert', split_axis=0, concat_axis=1, tiled=True)  29.1 us
    all_to_all x1, waiting for transfers between devices, shards(): lax.all_to_all(jnp.stack([scored] * lax.axis_size(('expert', 'tensor'))),...  27.4 us
  transfers between devices with their start and end apart: 5, of which 4 were waited for; matrix products, arithmetic and copies ran while one was open for 3% of the time, Pallas kernels for 0%

profile of v1, /device:TPU:1, one launch (start us, length us, event | category | flops | bytes accessed | tf_op | source)
XLA Modules:
  0.0 543.9 jit_solution(5455059789102198824)
XLA Ops:
  7.2 0.9 copy.21
  8.1 0.3 convert_reduce_fusion
  8.4 0.2 reduce_window_sum.11
  8.6 2.4 select_reduce_fusion
  11.0 1.2 fusion
  12.2 0.3 convolution_convert_fusion.1
  12.6 29.1 %all_to_all.26 = bf16[16,64,160]{2,1,0:T(8,128)(2,1)S(1)} all-to-all(bf16[16,64,160]{2,1,0:T(8,128)(2,1)S(1)} %convolution_convert_fusion.1), channel_id=1, replica_groups=mesh['expert'=16,'tensor'=32] {'expert'}, dimensions={0} | all-to-all | bytes 655360 | tf_op jit(solution)/shard_map/all_to_all | solution.py:46
  41.7 0.9 copy.24
  42.7 110.4 %all-gather.6.cloned.1.call-done = bf16[1024,5120]{0,1:T(8,128)(2,1)} async-done(((bf16[1024,160]{0,1:T(8,128)(2,1)}), bf16[1024,5120]{0,1:T(8,128)(2,1)}) %all-gather.6.cloned.1.call-update) | async-done | bytes 10485776 | tf_op jit(solution)/shard_map/all_gather | solution.py:50
  153.1 6.1 %fusion.11 = f32[1024,48]{0,1:T(8,128)S(1)} fusion(bf16[1024,5120]{0,1:T(8,128)(2,1)} %all-gather.6.cloned.1.call-done, bf16[1,48,5120]{2,1,0:T(8,128)(2,1)S(1)} %copy-done.3), kind=kOutput, calls=%fused_computation.24 | convolution fusion | flops 503316480 | bytes 11173888 | tf_op jit(solution)/shard_map/erw,efw->erf/dot_general | solution.py:55
  159.2 0.9 copy-done.1
  160.1 2.6 fusion.2
  162.7 0.2 all-gather.4.cloned.1.call-start
  162.9 0.5 all-gather.4.cloned.1.call-update
  163.5 0.1 copy.22
  163.6 2.7 convolution_bitcast_fusion
  166.3 76.0 %all-gather.8.cloned.1.call-done = bf16[1024,1536]{0,1:T(8,128)(2,1)} async-done(((bf16[1024,48]{0,1:T(8,128)(2,1)}), bf16[1024,1536]{0,1:T(8,128)(2,1)}) %all-gather.8.cloned.1.call-update) | async-done | bytes 3145744 | tf_op jit(solution)/shard_map/all_gather | solution.py:63
  242.3 2.6 fusion.1
  244.9 0.8 copy.25
  245.8 0.5 broadcast.30
  246.3 4.0 reduce.1
  250.3 1.5 reshape.76
  251.9 11.8 %all-to-all-start.1 = ((bf16[16,2,5120]{2,1,0:T(2,128)(2,1)}), bf16[16,2,5120]{2,1,0:T(2,128)(2,1)S(1)}, u32[]{:S(2)}, u32[]{:S(2)}) async-start(bf16[16,2,5120]{2,1,0:T(2,128)(2,1)} %reshape.76), calls=%async_computation.1 | async-start | bytes 655360 | tf_op jit(solution)/shard_map/all_to_all | solution.py:70
  263.6 59.9 %all-gather.4.cloned.1.call-done = bf16[128,5120]{0,1:T(8,128)(2,1)} async-done(((bf16[128,160]{0,1:T(8,128)(2,1)}), bf16[128,5120]{0,1:T(8,128)(2,1)}) %all-gather.4.cloned.1.call-update) | async-done | bytes 1310736 | tf_op jit(solution)/shard_map/all_gather | solution.py:51
  323.6 1.8 fusion.21
  325.4 0.4 fusion.5
  325.7 36.7 %all_gather.13 = bf16[128,1536]{0,1:T(8,128)(2,1)S(1)} all-gather(bf16[128,48]{0,1:T(8,128)(2,1)S(1)} %fusion.5), channel_id=1, replica_groups=mesh['expert'=16,'tensor'=32] {'tensor'}, dimensions={1}, use_global_device_ids=true | all-gather | bytes 405504 | tf_op jit(solution)/shard_map/all_gather | solution.py:64
  362.4 0.9 reshape.77
  363.4 0.1 copy.32
  363.5 1.1 copy-done.5
  364.6 1.1 convolution_bitcast_fusion.1
  365.7 0.3 fusion.4
  366.0 0.1 slice.4
  366.1 0.1 copy.29
  366.2 0.1 stack_reshape.2
  366.3 0.7 stack.3
  367.0 4.6 reduce.2
  371.6 1.5 reshape.78
  373.2 31.1 %all-to-all-start.2 = ((bf16[512,2,320]{2,1,0:T(2,128)(2,1)}), bf16[512,2,320]{2,1,0:T(2,128)(2,1)S(1)}, u32[]{:S(2)}, u32[]{:S(2)}) async-start(bf16[512,2,320]{2,1,0:T(2,128)(2,1)} %reshape.78), calls=%async_computation.2 | async-start | bytes 1572864 | tf_op jit(solution)/shard_map/all_to_all | solution.py:79
  404.3 27.4 %all-to-all-done.2 = bf16[512,2,320]{2,1,0:T(2,128)(2,1)S(1)} async-done(((bf16[512,2,320]{2,1,0:T(2,128)(2,1)}), bf16[512,2,320]{2,1,0:T(2,128)(2,1)S(1)}, u32[]{:S(2)}, u32[]{:S(2)}) %all-to-all-start.2) | async-done | bytes 655392 | tf_op jit(solution)/shard_map/all_to_all | solution.py:79
  431.7 1.1 reshape.79
  432.9 4.8 reduce
  437.7 2.8 reshape_reshape.3
  440.5 0.2 copy.30
  440.7 1.7 reshape.71
  442.4 0.7 exponential_reduce_fusion
  443.1 93.7 %all-reduce = (f32[64]{0:T(128)S(1)}, f32[64]{0:T(128)S(1)}) all-reduce(f32[64]{0:T(128)S(1)} %get-tuple-element.3, f32[64]{0:T(128)S(1)} %get-tuple-element.2), channel_id=1, replica_groups=mesh['expert'=16,'tensor'=32] {'expert','tensor'}, use_global_device_ids=true, to_apply=%region_4.5 | all-reduce | flops 128 | bytes 1024 | tf_op jit(solution)/shard_map/psum | solution.py:94
  536.8 0.5 log_subtract_fusion
  (35 shorter events, 0.2 us)
Async XLA Ops:
  7.2 435.2 %copy-start = (bf16[128,5120]{1,0:T(8,128)(2,1)S(1)}, bf16[128,5120]{1,0:T(8,128)(2,1)}, u32[]{:S(2)}) copy-start(bf16[128,5120]{1,0:T(8,128)(2,1)} %param.20) | copy-start | bytes 3932164
  7.2 145.9 %all-gather.6.cloned.1.call-start = ((), (), s32[]{:S(2)}) async-start(), calls=%async_computation.4 | async-start | bytes 10813440 | tf_op jit(solution)/shard_map/all_gather | solution.py:50
  8.4 3.8 copy-start.10
  12.6 140.5 %copy-start.3 = (bf16[1,48,5120]{2,1,0:T(8,128)(2,1)S(1)}, bf16[1,48,5120]{2,1,0:T(8,128)(2,1)}, u32[]{:S(2)}) copy-start(bf16[1,48,5120]{2,1,0:T(8,128)(2,1)} %param.14) | copy-start | bytes 1474564
  42.6 116.5 %copy-start.4 = (bf16[1,48,5120]{2,1,0:T(8,128)(2,1)S(1)}, bf16[1,48,5120]{2,1,0:T(8,128)(2,1)}, u32[]{:S(2)}) copy-start(bf16[1,48,5120]{2,1,0:T(8,128)(2,1)} %param.15) | copy-start | bytes 1474564
  42.6 199.7 %all-gather.8.cloned.1.call-start = ((), (), s32[]{:S(2)}) async-start(), calls=%async_computation.5 | async-start | bytes 3244032 | tf_op jit(solution)/shard_map/all_gather | solution.py:63
  153.1 7.0 %copy-start.1 = (bf16[1024,5120]{0,1:T(8,128)(2,1)S(1)}, bf16[1024,5120]{0,1:T(8,128)(2,1)}, u32[]{:S(2)}) copy-start(bf16[1024,5120]{0,1:T(8,128)(2,1)} %all-gather.6.cloned.1.call-done) | copy-start | bytes 31457284
  160.1 3.4 copy-start.13
  162.7 160.9 %all-gather.4.cloned.1.call-start = ((), (), s32[]{:S(2)}) async-start(), calls=%async_computation.3 | async-start | bytes 1351680 | tf_op jit(solution)/shard_map/all_gather | solution.py:51
  163.6 78.8 %copy-start.8 = (bf16[1,1536,160]{1,2,0:T(8,128)(2,1)S(1)}, bf16[1,1536,160]{1,2,0:T(8,128)(2,1)}, u32[]{:S(2)}) copy-start(bf16[1,1536,160]{1,2,0:T(8,128)(2,1)} %param.16) | copy-start | bytes 1474564
  250.3 73.2 %copy-start.6 = (bf16[48,5120]{1,0:T(8,128)(2,1)S(1)}, bf16[48,5120]{1,0:T(8,128)(2,1)}, u32[]{:S(2)}) copy-start(bf16[48,5120]{1,0:T(8,128)(2,1)} %param.17) | copy-start | bytes 1474564
  251.9 73.5 %copy-start.7 = (bf16[48,5120]{1,0:T(8,128)(2,1)S(1)}, bf16[48,5120]{1,0:T(8,128)(2,1)}, u32[]{:S(2)}) copy-start(bf16[48,5120]{1,0:T(8,128)(2,1)} %param.18) | copy-start | bytes 1474564
  251.9 110.6 %all-to-all-start.1 = ((bf16[16,2,5120]{2,1,0:T(2,128)(2,1)}), bf16[16,2,5120]{2,1,0:T(2,128)(2,1)S(1)}, u32[]{:S(2)}, u32[]{:S(2)}) async-start(bf16[16,2,5120]{2,1,0:T(2,128)(2,1)} %reshape.76), calls=%async_computation.1 | async-start | bytes 655360 | tf_op jit(solution)/shard_map/all_to_all | solution.py:70
  323.6 1.8 copy-start.2
  363.4 1.2 copy-start.5
  363.4 2.4 copy-start.9
  363.4 2.4 copy-start.11
  366.0 5.6 %copy-start.12 = (bf16[128,160]{0,1:T(8,128)(2,1)}, bf16[128,160]{0,1:T(8,128)(2,1)S(1)}, u32[]{:S(2)}) copy-start(bf16[128,160]{0,1:T(8,128)(2,1)S(1)} %fusion.4) | copy-start | bytes 122884
  373.2 58.5 %all-to-all-start.2 = ((bf16[512,2,320]{2,1,0:T(2,128)(2,1)}), bf16[512,2,320]{2,1,0:T(2,128)(2,1)S(1)}, u32[]{:S(2)}, u32[]{:S(2)}) async-start(bf16[512,2,320]{2,1,0:T(2,128)(2,1)} %reshape.78), calls=%async_computation.2 | async-start | bytes 1572864 | tf_op jit(solution)/shard_map/all_to_all | solution.py:79
  440.7 1.7 copy-start.14
Sparse Core Ops, SparseCore 0:
  42.7 110.3 all-gather.5
  162.8 79.4 all-gather.7
  245.5 78.0 all-gather.3
